TPU v7x, 128 devices: a whole 4x4x4 slice. The times are simulated.
128 devices in a mesh: oct: 2 (over core), sub: 64 (over x, z, y).
Axes of the slice: x: 4, y: 4, z: 4, core: 2. Of those that a mesh axis runs over, the one named last changes fastest.
Arguments:
- coefficients: float32 [2048, 4096], P(('oct', 'sub')), may hold values from -6 to 6
- potential: float32 [2048, 4096], P(('oct', 'sub')), may hold values from 0.2 to 2
- to_values: float32 [16, 16], replicated, may hold values from -1.5 to 1.5
- x_kernels: bfloat16 [20, 48, 16], replicated, may hold values from -0.5 to 0.5
- yz_kernels: bfloat16 [256, 46080], replicated, may hold values from -0.046875 to 0.046875
- two_scale: float32 [2, 16, 16], replicated, may hold values from -1 to 1
- disp_ids: int32 [2048, 16], P(('oct', 'sub')), may hold values from -1 to 26, as said below
- dest_box: int32 [2048, 16], P(('oct', 'sub')), may hold values from -1 to 2047, as said below
- parent_of: int32 [2048], P(('oct', 'sub')), may hold values from 0 to 255, as said below
- child_octant: int32 [2048], P(('oct', 'sub')), may hold values from 0 to 7
Outputs:
- next_field: float32 [2048, 4096], P(('oct', 'sub'))
- parents: float32 [256, 4096], P(('oct', 'sub'))
Inputs may be any that keep to these rules, and one draw needn't show every extreme that they name: `disp_ids`: -1 marks an empty slot, exactly where dest_box is -1; in every row the live slots come first, 4 or more of them. `dest_box`: among the live slots of one aligned block of 16 rows, at most 2 name boxes of any one aligned block of 16 boxes; some box block receives exactly 2 from every row block. Every parent is named by exactly 8 boxes, whose child_octant values are 0 to 7; parent_of[b] // 128 == b // 1024. Within one aligned block of 16 boxes, at most 1 box has its parent in any one aligned block of 2 parents, and some parent block is named by exactly 1 of them.
All inputs are finite; a program needn't handle non-finite values.
Results may differ from a plain program's by a relative error of at most 0.018.
Values may be sent and summed in bfloat16 or wider, within the bound.
A program may use at most 192 MiB of HBM per device.

v0:
```python
import jax
import jax.numpy as jnp
from jax import lax
from jax.sharding import PartitionSpec as P

ITERS = 2


def apply_pair(blocks, along_x, pair, order_k):
    highest = lax.Precision.HIGHEST
    rows_total = blocks.shape[0]
    plane_size = order_k * order_k
    inner = jnp.dot(blocks.reshape(rows_total * order_k, plane_size), pair, precision=highest)
    inner = inner.reshape(rows_total, order_k, plane_size)
    return jnp.einsum("ix,bxr->bir", along_x, inner, precision=highest).reshape(
        rows_total, plane_size * order_k
    )


def quad_of(filters):
    order_k = filters.shape[1]
    return jnp.einsum("cjy,dkz->yzcdjk", filters, filters, precision=lax.Precision.HIGHEST).reshape(
        order_k * order_k, 4 * order_k * order_k
    )


def lift_boxes(blocks, filters, quad, octant):
    highest = lax.Precision.HIGHEST
    rows_total = blocks.shape[0]
    order_k = filters.shape[1]
    plane_size = order_k * order_k
    inner = jnp.dot(blocks.reshape(rows_total * order_k, plane_size), quad, precision=highest)
    inner = inner.reshape(rows_total, order_k, 4, plane_size)
    select = (octant[:, None] % 4 == jnp.arange(4)[None, :]).astype(jnp.float32)
    inner = jnp.einsum("bxcr,bc->bxr", inner, select, precision=highest)
    along_x = jnp.where((octant // 4 == 1)[:, None, None], filters[1][None], filters[0][None])
    return jnp.einsum("bix,bxr->bir", along_x, inner, precision=highest).reshape(
        rows_total, plane_size * order_k
    )


def shards(
    coefficients,
    potential,
    to_values,
    x_kernels,
    yz_kernels,
    two_scale,
    disp_ids,
    dest_box,
    parent_of,
    child_octant,
):
    highest = lax.Precision.HIGHEST
    box_count = coefficients.shape[0]
    order_k = to_values.shape[0]
    plane_size = order_k * order_k
    cube_size = plane_size * order_k
    slot_count = disp_ids.shape[1]
    term_count = x_kernels.shape[0]
    oct_count = lax.axis_size("oct")
    sub_count = lax.axis_size("sub")
    devices_all = oct_count * sub_count
    capacity = box_count * slot_count // devices_all
    block_boxes = 16
    count_blocks = box_count // block_boxes
    parent_local = box_count // 8
    per_group = sub_count * parent_local
    value_pair = jnp.einsum("jy,kz->yzjk", to_values, to_values, precision=highest).reshape(
        plane_size, plane_size
    )
    back_pair = jnp.einsum("yj,zk->yzjk", to_values, to_values, precision=highest).reshape(
        plane_size, plane_size
    )
    flipped = jnp.swapaxes(two_scale, 1, 2)
    lift_quad = quad_of(two_scale)
    drop_quad = quad_of(flipped)
    flat_dest = dest_box.reshape(-1)
    owner_ids = flat_dest // box_count
    is_live = flat_dest >= 0
    hits = (owner_ids[:, None] == jnp.arange(devices_all, dtype=jnp.int32)[None, :]).astype(
        jnp.int32
    )
    before = jnp.cumsum(hits, axis=0) - hits
    rank_ids = jnp.sum(before * hits, axis=1)
    slot_index = jnp.where(is_live, owner_ids * capacity + rank_ids, devices_all * capacity)
    local_box = flat_dest - owner_ids * box_count
    label_row = (
        jnp.zeros((devices_all * capacity + 1,), jnp.bfloat16)
        .at[slot_index]
        .set(local_box.astype(jnp.bfloat16))[:-1]
    )
    local_parents = parent_of - lax.axis_index("oct") * per_group
    member_up = (jnp.arange(per_group, dtype=jnp.int32)[:, None] == local_parents[None, :]).astype(
        jnp.float32
    )
    box_ids = jnp.arange(box_count, dtype=jnp.int32)

    def convolve(carry_none, block_items):
        source_blk, disp_blk = block_items
        partial_value = jnp.dot(
            source_blk.reshape(block_boxes * order_k, plane_size),
            yz_kernels,
            preferred_element_type=jnp.float32,
        ).astype(jnp.bfloat16)
        partial_value = partial_value.reshape(block_boxes, order_k, term_count, 9 * plane_size)
        convolved = jnp.einsum(
            "bxmr,max->bar", partial_value, x_kernels, preferred_element_type=jnp.float32
        )
        convolved = (
            convolved.reshape(block_boxes, 3, order_k, 9, plane_size)
            .transpose(0, 1, 3, 2, 4)
            .reshape(block_boxes, 27, cube_size)
        )
        picked = jnp.take_along_axis(
            convolved, jnp.maximum(disp_blk, 0)[:, :, None], axis=1
        ).astype(jnp.bfloat16)
        return (carry_none, picked)

    current = coefficients
    own_parents = jnp.zeros((parent_local, cube_size), jnp.float32)
    for iteration in range(ITERS):
        values = apply_pair(current, to_values, value_pair, order_k)
        product = values * (potential + 0.25 * values * values)
        source = apply_pair(product, to_values.T, back_pair, order_k).astype(jnp.bfloat16)
        unused, picked = lax.scan(
            convolve,
            jnp.zeros((), jnp.int32),
            (
                source.reshape(count_blocks, block_boxes, cube_size),
                disp_ids.reshape(count_blocks, block_boxes, slot_count),
            ),
        )
        outgoing = picked.reshape(box_count * slot_count, cube_size)
        send_tiles = (
            jnp.zeros((devices_all * capacity + 1, cube_size), jnp.bfloat16)
            .at[slot_index]
            .set(outgoing)[:-1]
        )
        arrived, arrived_labels = (
            lax.all_to_all(
                send_tiles.reshape(devices_all, capacity, cube_size),
                ("oct", "sub"),
                split_axis=0,
                concat_axis=0,
                tiled=True,
            ),
            lax.all_to_all(
                label_row.reshape(devices_all, capacity),
                ("oct", "sub"),
                split_axis=0,
                concat_axis=0,
                tiled=True,
            ),
        )
        incoming = arrived.reshape(devices_all * capacity, cube_size)
        arrived_boxes = arrived_labels.reshape(-1).astype(jnp.int32)
        member_in = (arrived_boxes[None, :] == box_ids[:, None]).astype(jnp.bfloat16)
        gathered = jnp.dot(member_in, incoming, preferred_element_type=jnp.float32)
        lifted = lift_boxes(gathered, two_scale, lift_quad, child_octant)
        contrib = jnp.dot(member_up, lifted, precision=highest)
        own_parents = lax.psum_scatter(contrib, "sub", scatter_dimension=0, tiled=True)
        everyone = lax.all_gather(
            own_parents.astype(jnp.bfloat16), "sub", axis=0, tiled=True
        ).astype(own_parents.dtype)
        matched = jnp.take(everyone, local_parents, axis=0)
        current = gathered - lift_boxes(matched, flipped, drop_quad, child_octant)
    return (current, own_parents)


def solution(mesh):
    placed = (
        P(("oct", "sub"), None),
        P(("oct", "sub"), None),
        P(),
        P(),
        P(),
        P(),
        P(("oct", "sub"), None),
        P(("oct", "sub"), None),
        P(("oct", "sub")),
        P(("oct", "sub")),
    )
    return jax.shard_map(
        shards,
        mesh=mesh,
        in_specs=placed,
        out_specs=(P(("oct", "sub"), None), P(("oct", "sub"), None)),
        check_vma=False,
    )
```

profile of v0, /device:TPU:0, one launch (start us, length us, event | category | flops | bytes accessed | tf_op | source)
XLA Modules:
  0.0 983.5 jit_solution(8387002277231726505)
XLA Ops:
  7.2 0.8 reshape.309
  7.9 0.8 reshape.308
  10.2 2.2 scatter_custom_fusion
  12.3 0.8 all_to_all.17
  13.1 11.9 %all-to-all-start = ((bf16[128,1,2]{2,1,0:T(2,128)(2,1)}), bf16[128,1,2]{2,1,0:T(2,128)(2,1)}, u32[]{:S(2)}, u32[]{:S(2)}) async-start(bf16[128,1,2]{2,1,0:T(2,128)(2,1)} %all_to_all.17), calls=%async_computation | async-start | bytes 131072 | tf_op jit(solution)/shard_map/all_to_all | solution.py:148
  25.1 1.3 shift-left_or_fusion
  27.1 2.5 multiply_bitcast_fusion.2
  29.5 2.5 reshape.430
  33.2 0.9 reshape.409
  35.0 20.6 %convolution_convert_fusion.1 = bf16[256,46080]{1,0:T(8,128)(2,1)} fusion(bf16[256,256]{1,0:T(8,128)(2,1)S(1)} %bitcast.221, bf16[256,46080]{1,0:T(8,128)(2,1)} %param.18), kind=kOutput, calls=%fused_computation.8 | convolution fusion | flops 6051594240 | bytes 47316992 | tf_op jit(solution)/shard_map/while/body/eval_jaxpr/dot_general | solution.py:101
  55.6 32.9 %reshape.316 = bf16[16,16,20,2304]{3,2,1,0:T(8,128)(2,1)} reshape(bf16[256,46080]{1,0:T(8,128)(2,1)} %convolution_convert_fusion.1) | data formatting | bytes 47185920 | tf_op jit(solution)/shard_map/while/body/eval_jaxpr/reshape | solution.py:106
  88.5 11.5 %convolution_bitcast_fusion.1 = bf16[16,48,2304]{2,1,0:T(8,128)(2,1)S(1)} fusion(bf16[16,16,20,2304]{3,2,1,0:T(8,128)(2,1)} %reshape.316, bf16[20,48,16]{1,2,0:T(8,128)(2,1)} %param.17), kind=kOutput, calls=%fused_computation.12 | convolution fusion | flops 1132462080 | bytes 27162624 | tf_op jit(solution)/shard_map/while/body/eval_jaxpr/bxmr,max->bar/dot_general | solution.py:107
  100.0 4.9 reshape.317
  104.9 6.0 copy.44
  110.9 5.4 reshape.318
  117.1 8.5 gather_fusion
  125.6 3.5 select_convert_fusion.1
  129.1 5.1 scatter_custom_fusion.1
  134.2 1.5 slice.49
  135.7 4.5 reshape.320
  140.2 9.9 %all-to-all-start.1 = ((bf16[128,2,4096]{2,1,0:T(2,128)(2,1)}), bf16[128,2,4096]{2,1,0:T(2,128)(2,1)S(1)}, u32[]{:S(2)}, u32[]{:S(2)}) async-start(bf16[128,2,4096]{2,1,0:T(2,128)(2,1)} %reshape.320), calls=%async_computation.1 | async-start | bytes 4194304 | tf_op jit(solution)/shard_map/all_to_all | solution.py:141
  150.2 4.4 multiply_bitcast_fusion.1
  154.6 8.7 reshape.322
  163.3 1.6 copy.78
  166.5 1.1 convert_reduce_fusion
  167.7 12.3 %all-to-all-done.1 = bf16[128,2,4096]{2,1,0:T(2,128)(2,1)S(1)} async-done(((bf16[128,2,4096]{2,1,0:T(2,128)(2,1)}), bf16[128,2,4096]{2,1,0:T(2,128)(2,1)S(1)}, u32[]{:S(2)}, u32[]{:S(2)}) %all-to-all-start.1) | async-done | bytes 2097184 | tf_op jit(solution)/shard_map/all_to_all | solution.py:141
  180.0 2.2 reshape.321
  182.2 2.0 fusion.73
  184.2 1.0 fusion.32
  185.3 1.7 fusion.10
  187.6 1.0 fusion.55
  188.6 366.1 %all-reduce.6 = bf16[128,4096]{1,0:T(8,128)(2,1)S(1)} all-reduce(f32[128,4096]{1,0:T(8,128)S(1)} %fusion.55), channel_id=2, replica_groups=mesh['oct'=2,'sub'=64] {'sub'}, use_global_device_ids=true, to_apply=%region_5.7.clone | all-reduce | flops 524288 | bytes 3145728
  555.4 4.4 multiply_bitcast_fusion
  559.8 8.0 reshape.324
  568.4 45.9 %all-gather.5.cloned.1.call-done = bf16[64,2,4096]{2,1,0:T(2,128)(2,1)} async-done(((bf16[1,2,4096]{2,1,0:T(2,128)(2,1)}), bf16[64,2,4096]{2,1,0:T(2,128)(2,1)}) %all-gather.5.cloned.1.call-update) | async-done | bytes 1048592 | tf_op jit(solution)/shard_map/all_gather | solution.py:163
  614.3 1.4 reshape.394
  615.6 1.3 gather_fusion.1
  617.0 1.0 broadcast_select_fusion.1
  618.1 1.0 fusion.28
  619.2 1.7 fusion.8
  623.5 20.6 %convolution_convert_fusion = bf16[256,46080]{1,0:T(8,128)(2,1)} fusion(bf16[256,256]{1,0:T(8,128)(2,1)S(1)} %bitcast.222, bf16[256,46080]{1,0:T(8,128)(2,1)} %param.18), kind=kOutput, calls=%fused_computation.7 | convolution fusion | flops 6051594240 | bytes 47316992 | tf_op jit(solution)/shard_map/while/body/eval_jaxpr/dot_general | solution.py:101
  644.1 32.9 %reshape.327 = bf16[16,16,20,2304]{3,2,1,0:T(8,128)(2,1)} reshape(bf16[256,46080]{1,0:T(8,128)(2,1)} %convolution_convert_fusion) | data formatting | bytes 47185920 | tf_op jit(solution)/shard_map/while/body/eval_jaxpr/reshape | solution.py:106
  677.0 11.5 %convolution_bitcast_fusion = bf16[16,48,2304]{2,1,0:T(8,128)(2,1)S(1)} fusion(bf16[16,16,20,2304]{3,2,1,0:T(8,128)(2,1)} %reshape.327, bf16[20,48,16]{1,2,0:T(8,128)(2,1)} %param.17), kind=kOutput, calls=%fused_computation.11 | convolution fusion | flops 1132462080 | bytes 27162624 | tf_op jit(solution)/shard_map/while/body/eval_jaxpr/bxmr,max->bar/dot_general | solution.py:107
  688.6 5.1 reshape.328
  693.7 6.0 copy.55
  699.7 5.1 reshape.329
  704.8 8.5 gather_fusion.2
  713.3 3.5 select_convert_fusion
  716.8 5.3 scatter_custom_fusion.2
  722.2 1.5 slice.52
  723.6 3.2 reshape.331
  726.8 36.1 %all_to_all.21 = bf16[128,2,4096]{2,1,0:T(2,128)(2,1)} all-to-all(bf16[128,2,4096]{2,1,0:T(2,128)(2,1)S(1)} %reshape.331), channel_id=1, replica_groups=mesh['oct'=2,'sub'=64] {'oct','sub'}, dimensions={0} | all-to-all | bytes 4194304 | tf_op jit(solution)/shard_map/all_to_all | solution.py:141
  763.0 2.7 reshape.332
  767.0 1.0 fusion.24
  768.0 1.7 fusion.6
  770.3 2.3 fusion.54
  772.7 130.4 %all-reduce.5.cloned.1.call-done = f32[128,4096]{1,0:T(8,128)} async-done(((f32[128,4096]{1,0:T(8,128)}), f32[128,4096]{1,0:T(8,128)}) %all-reduce.5.cloned.1.call-update) | async-done | bytes 2097168
  903.1 1.5 convert_bitcast_fusion
  904.7 63.3 %all-gather.7.cloned.1.call-done = bf16[64,2,4096]{2,1,0:T(2,128)(2,1)} async-done(((bf16[1,2,4096]{2,1,0:T(2,128)(2,1)}), bf16[64,2,4096]{2,1,0:T(2,128)(2,1)}) %all-gather.7.cloned.1.call-update) | async-done | bytes 1048592 | tf_op jit(solution)/shard_map/all_gather | solution.py:163
  968.0 1.6 reshape.395
  969.6 1.6 gather_fusion.3
  971.2 1.0 broadcast_select_fusion
  972.4 1.0 fusion.20
  973.4 1.7 fusion.4
  (142 shorter events, 13.7 us)
Async XLA Ops:
  10.2 16.2 %copy-start.32 = (s32[256,1]{0,1:T(1,128)}, s32[256,1]{0,1:T(1,128)S(1)}, u32[]{:S(2)}) copy-start(s32[256,1]{0,1:T(1,128)S(1)} %compare_select_fusion.1) | copy-start | bytes 3076
  13.1 127.0 %all-to-all-start = ((bf16[128,1,2]{2,1,0:T(2,128)(2,1)}), bf16[128,1,2]{2,1,0:T(2,128)(2,1)}, u32[]{:S(2)}, u32[]{:S(2)}) async-start(bf16[128,1,2]{2,1,0:T(2,128)(2,1)} %all_to_all.17), calls=%async_computation | async-start | bytes 131072 | tf_op jit(solution)/shard_map/all_to_all | solution.py:148
  27.1 98.5 %copy-start.21 = (pred[16,16]{1,0:T(8,128)(4,1)}, pred[16,16]{1,0:T(8,128)(4,1)S(1)}, u32[]{:S(2)}) copy-start(pred[16,16]{1,0:T(8,128)(4,1)S(1)} %and_bitcast_fusion) | copy-start | bytes 772
  29.5 2.5 copy-start.11
  29.5 3.0 copy-start.10
  29.5 3.5 copy-start.8
  32.1 2.1 copy-start.4
  34.2 21.4 %copy-start.6 = (f32[256,256,1]{1,0,2:T(8,128)}, f32[256,256,1]{1,0,2:T(8,128)S(1)}, u32[]{:S(2)}) copy-start(f32[256,256,1]{1,0,2:T(8,128)S(1)} %reshape.409) | copy-start | bytes 786436
  140.2 10.0 %copy-start.12 = (f32[2,16,16]{2,1,0:T(8,128)S(1)}, f32[2,16,16]{2,1,0:T(8,128)}, u32[]{:S(2)}) copy-start(f32[2,16,16]{2,1,0:T(8,128)} %param.19) | copy-start | bytes 6148
  140.2 39.8 %all-to-all-start.1 = ((bf16[128,2,4096]{2,1,0:T(2,128)(2,1)}), bf16[128,2,4096]{2,1,0:T(2,128)(2,1)S(1)}, u32[]{:S(2)}, u32[]{:S(2)}) async-start(bf16[128,2,4096]{2,1,0:T(2,128)(2,1)} %reshape.320), calls=%async_computation.1 | async-start | bytes 4194304 | tf_op jit(solution)/shard_map/all_to_all | solution.py:141
  150.1 464.2 %all-gather.5.cloned.1.call-start = ((), (), s32[]{:S(2)}) async-start(), calls=%async_computation.3 | async-start | bytes 1064960 | tf_op jit(solution)/shard_map/all_gather | solution.py:163
  154.6 10.3 %copy-start.35 = (u32[128]{0:T(128)S(1)}, u32[128]{0:T(128)}, u32[]{:S(2)}) copy-start(u32[128]{0:T(128)} %constant.167) | copy-start | bytes 1540
  154.6 11.7 %copy-start.34 = (s32[16]{0:T(128)S(1)}, s32[16]{0:T(128)}, u32[]{:S(2)}) copy-start(s32[16]{0:T(128)} %param.23) | copy-start | bytes 196
  154.6 11.7 %copy-start.33 = (s32[16]{0:T(128)S(1)}, s32[16]{0:T(128)}, u32[]{:S(2)}) copy-start(s32[16]{0:T(128)} %param.22) | copy-start | bytes 196
  164.9 19.3 %copy-start = (f32[1024,256]{1,0:T(8,128)}, f32[1024,256]{1,0:T(8,128)S(1)}, u32[]{:S(2)}) copy-start(f32[1024,256]{1,0:T(8,128)S(1)} %copy.78) | copy-start | bytes 3145732
  166.3 454.5 %copy-start.25 = (pred[16]{0:T(512)(128)(4,1)}, pred[16]{0:T(512)(128)(4,1)S(1)}, u32[]{:S(2)}) copy-start(pred[16]{0:T(512)(128)(4,1)S(1)} %fusion.85) | copy-start | bytes 52
  166.4 402.0 %copy-start.30 = (s32[16]{0:T(128)}, s32[16]{0:T(128)S(1)}, u32[]{:S(2)}) copy-start(s32[16]{0:T(128)S(1)} %get-tuple-element.37) | copy-start | bytes 196
  166.4 450.6 %copy-start.28 = (pred[16]{0:T(512)(128)(4,1)}, pred[16]{0:T(512)(128)(4,1)S(1)}, u32[]{:S(2)}) copy-start(pred[16]{0:T(512)(128)(4,1)S(1)} %get-tuple-element.36) | copy-start | bytes 52
  166.5 20.5 %copy-start.17 = (f32[16,16]{1,0:T(8,128)}, f32[16,16]{1,0:T(8,128)S(1)}, u32[]{:S(2)}) copy-start(f32[16,16]{1,0:T(8,128)S(1)} %get-tuple-element.48) | copy-start | bytes 3076
  166.5 20.5 %copy-start.19 = (f32[16,16]{1,0:T(8,128)}, f32[16,16]{1,0:T(8,128)S(1)}, u32[]{:S(2)}) copy-start(f32[16,16]{1,0:T(8,128)S(1)} %get-tuple-element.49) | copy-start | bytes 3076
  167.7 16.5 %copy-start.23 = (s32[256]{0:T(256)}, s32[256]{0:T(256)S(1)}, u32[]{:S(2)}) copy-start(s32[256]{0:T(256)S(1)} %reshape.335) | copy-start | bytes 3076
  555.3 347.8 %all-reduce.5.cloned.1.call-start = ((), (), s32[]{:S(2)}) async-start(), calls=%async_computation.5 | async-start | bytes 4194304
  568.2 49.9 %copy-start.2 = (f32[1024,256]{1,0:T(8,128)}, f32[1024,256]{1,0:T(8,128)S(1)}, u32[]{:S(2)}) copy-start(f32[1024,256]{1,0:T(8,128)S(1)} %copy.79) | copy-start | bytes 3145732
  568.3 52.6 %copy-start.13 = (f32[16,16]{1,0:T(8,128)}, f32[16,16]{1,0:T(8,128)S(1)}, u32[]{:S(2)}) copy-start(f32[16,16]{1,0:T(8,128)S(1)} %copy.45) | copy-start | bytes 3076
  568.3 52.5 %copy-start.15 = (f32[16,16]{1,0:T(8,128)}, f32[16,16]{1,0:T(8,128)S(1)}, u32[]{:S(2)}) copy-start(f32[16,16]{1,0:T(8,128)S(1)} %copy.46) | copy-start | bytes 3076
  568.4 48.6 %copy-start.27 = (s32[1024]{0:T(1024)}, s32[1024]{0:T(1024)S(1)}, u32[]{:S(2)}) copy-start(s32[1024]{0:T(1024)S(1)} %pad_clamp_fusion) | copy-start | bytes 12292
  619.2 2.5 copy-start.5
  620.9 1.7 copy-start.9
  621.5 1.2 copy-start.7
  704.8 8.6 copy-start.22
  763.0 2.8 copy-start.24
  765.7 1.2 copy-start.1
  766.1 3.6 copy-start.18
  766.1 3.6 copy-start.20
  766.1 3.6 copy-start.26
  767.0 3.4 copy-start.31
  772.6 195.3 %all-gather.7.cloned.1.call-start = ((), (), s32[]{:S(2)}) async-start(), calls=%async_computation.4 | async-start | bytes 1064960 | tf_op jit(solution)/shard_map/all_gather | solution.py:163
  904.7 66.5 %copy-start.29 = (pred[16]{0:T(512)(128)(4,1)S(1)}, pred[16]{0:T(512)(128)(4,1)}, u32[]{:S(2)}) copy-start(pred[16]{0:T(512)(128)(4,1)} %copy-done.28) | copy-start | bytes 52
  969.6 2.7 copy-start.3
  972.2 2.9 copy-start.14
  972.3 2.9 copy-start.16
Sparse Core Ops, SparseCore 0:
  555.5 58.7 all-gather.4
  772.7 130.3 all-reduce.4
  906.6 61.3 all-gather.6
where the time goes:
time: 990 us; the launch traced here: 983 us
  blocking collectives  402 us (41%)
  waiting for transfers between devices  252 us (25%)
  local copies, waits for them, and re-layouts  180 us (18%)
  matrix products  85.5 us (9%)
  other arithmetic  26.4 us (3%)
  starting transfers between devices  21.9 us (2%)
  between operations  15.8 us (2%)
    unnamed x1, blocking collectives  366 us
    unnamed x4, waiting for transfers between devices  130 us
    all_gather x2, waiting for transfers between devices, shards(): lax.all_gather(own_parents.astype(jnp.bfloat16), 'sub', axis=0, tiled=True)  109 us
    reshape x2, local copies, waits for them, and re-layouts, convolve(): partial_value.reshape(block_boxes, order_k, term_count, 9 * plane_size)  65.8 us
    dot_general x2, matrix products, convolve(): jnp.dot(source_blk.reshape(block_boxes * order_k, plane_size), yz_kernels...  41.2 us
    all_to_all x1, blocking collectives, shards(): lax.all_to_all(send_tiles.reshape(devices_all, capacity, cube_size), ('oc...  36.1 us
    dot_general x2, matrix products, convolve(): jnp.einsum('bxmr,max->bar', partial_value, x_kernels, preferred_element_t...  23.1 us
  transfers between devices with their start and end apart: 5, of which 4 were waited for; matrix products, arithmetic and copies ran while one was open for 15% of the time, Pallas kernels for 0%

commit v1 on v0

--- a/solution.py
+++ b/solution.py
@@ -160,8 +160,11 @@
         lifted = lift_boxes(gathered, two_scale, lift_quad, child_octant)
         contrib = jnp.dot(member_up, lifted, precision=highest)
         own_parents = lax.psum_scatter(contrib, "sub", scatter_dimension=0, tiled=True)
-        everyone = lax.all_gather(
-            own_parents.astype(jnp.bfloat16), "sub", axis=0, tiled=True
+        everyone = jnp.concatenate(
+            lax.all_to_all(
+                jnp.stack([own_parents.astype(jnp.bfloat16)] * lax.axis_size("sub")), "sub", 0, 0
+            ),
+            axis=0,
         ).astype(own_parents.dtype)
         matched = jnp.take(everyone, local_parents, axis=0)
         current = gathered - lift_boxes(matched, flipped, drop_quad, child_octant)

time: 990 us -> 916 us (0.925)
  waiting for transfers between devices: 252 us -> 144 us
  blocking collectives: 402 us -> 430 us
    all_gather x2 -> x0, waiting for transfers between devices: 109 us -> none  [shards(): lax.all_gather(own_parents.astype(jnp.bfloat16), 'sub', axis=0, tiled=True)]
    all_to_all x0 -> x1, blocking collectives: none -> 23.1 us  [shards(): lax.all_to_all(jnp.stack([own_parents.astype(jnp.bfloat16)] * lax.axis_si...]
    unnamed x4 -> x2, waiting for transfers between devices: 130 us -> 130 us
  transfers between devices with their start and end apart: 5 -> 4, of which waited for: 4 -> 3; matrix products, arithmetic and copies ran while one was open for 15% -> 16% of each run, Pallas kernels for 0% -> 0%
where the time goes in v1:
time: 916 us; the launch traced here: 910 us
  blocking collectives  430 us (47%)
  local copies, waits for them, and re-layouts  181 us (20%)
  waiting for transfers between devices  144 us (16%)
  matrix products  85.5 us (9%)
  starting transfers between devices  27.6 us (3%)
  other arithmetic  26.3 us (3%)
  between operations  15.9 us (2%)
    unnamed x1, blocking collectives  368 us
    unnamed x2, waiting for transfers between devices  130 us
    reshape x2, local copies, waits for them, and re-layouts, convolve(): partial_value.reshape(block_boxes, order_k, term_count, 9 * plane_size)  65.8 us
    dot_general x2, matrix products, convolve(): jnp.dot(source_blk.reshape(block_boxes * order_k, plane_size), yz_kernels...  41.2 us
    all_to_all x1, blocking collectives, shards(): lax.all_to_all(send_tiles.reshape(devices_all, capacity, cube_size), ('oc...  39.2 us
    all_to_all x1, blocking collectives, shards(): lax.all_to_all(jnp.stack([own_parents.astype(jnp.bfloat16)] * lax.axis_si...  23.1 us
    dot_general x2, matrix products, convolve(): jnp.einsum('bxmr,max->bar', partial_value, x_kernels, preferred_element_t...  23 us
  transfers between devices with their start and end apart: 4, of which 3 were waited for; matrix products, arithmetic and copies ran while one was open for 16% of the time, Pallas kernels for 0%

profile of v1, /device:TPU:0, one launch (start us, length us, event | category | flops | bytes accessed | tf_op | source)
XLA Modules:
  0.0 909.7 jit_solution(2773843601875598103)
XLA Ops:
  10.2 2.2 scatter_custom_fusion
  12.3 0.8 all_to_all.25
  13.1 12.2 %all-to-all-start = ((bf16[128,1,2]{2,1,0:T(2,128)(2,1)}), bf16[128,1,2]{2,1,0:T(2,128)(2,1)}, u32[]{:S(2)}, u32[]{:S(2)}) async-start(bf16[128,1,2]{2,1,0:T(2,128)(2,1)} %all_to_all.25), calls=%async_computation | async-start | bytes 131072 | tf_op jit(solution)/shard_map/all_to_all | solution.py:148
  25.4 1.3 shift-left_or_fusion
  27.4 2.4 multiply_bitcast_fusion.2
  29.8 2.5 reshape.436
  33.5 0.9 reshape.415
  35.3 20.6 %convolution_convert_fusion.1 = bf16[256,46080]{1,0:T(8,128)(2,1)} fusion(bf16[256,256]{1,0:T(8,128)(2,1)S(1)} %bitcast.217, bf16[256,46080]{1,0:T(8,128)(2,1)} %param.18), kind=kOutput, calls=%fused_computation.8 | convolution fusion | flops 6051594240 | bytes 47316992 | tf_op jit(solution)/shard_map/while/body/eval_jaxpr/dot_general | solution.py:101
  55.9 32.9 %reshape.326 = bf16[16,16,20,2304]{3,2,1,0:T(8,128)(2,1)} reshape(bf16[256,46080]{1,0:T(8,128)(2,1)} %convolution_convert_fusion.1) | data formatting | bytes 47185920 | tf_op jit(solution)/shard_map/while/body/eval_jaxpr/reshape | solution.py:106
  88.8 11.5 %convolution_bitcast_fusion.1 = bf16[16,48,2304]{2,1,0:T(8,128)(2,1)S(1)} fusion(bf16[16,16,20,2304]{3,2,1,0:T(8,128)(2,1)} %reshape.326, bf16[20,48,16]{1,2,0:T(8,128)(2,1)} %param.17), kind=kOutput, calls=%fused_computation.12 | convolution fusion | flops 1132462080 | bytes 27162624 | tf_op jit(solution)/shard_map/while/body/eval_jaxpr/bxmr,max->bar/dot_general | solution.py:107
  100.3 4.9 reshape.327
  105.2 6.0 copy.44
  111.2 5.3 reshape.328
  117.3 8.5 gather_fusion
  125.8 3.5 select_convert_fusion.1
  129.3 5.1 scatter_custom_fusion.1
  134.4 1.5 slice.49
  135.8 4.5 reshape.330
  140.3 9.9 %all-to-all-start.1 = ((bf16[128,2,4096]{2,1,0:T(2,128)(2,1)}), bf16[128,2,4096]{2,1,0:T(2,128)(2,1)S(1)}, u32[]{:S(2)}, u32[]{:S(2)}) async-start(bf16[128,2,4096]{2,1,0:T(2,128)(2,1)} %reshape.330), calls=%async_computation.1 | async-start | bytes 4194304 | tf_op jit(solution)/shard_map/all_to_all | solution.py:141
  150.3 4.4 multiply_bitcast_fusion.1
  154.7 8.7 reshape.332
  163.4 1.6 copy.78
  166.6 1.1 convert_reduce_fusion
  167.8 12.3 %all-to-all-done.1 = bf16[128,2,4096]{2,1,0:T(2,128)(2,1)S(1)} async-done(((bf16[128,2,4096]{2,1,0:T(2,128)(2,1)}), bf16[128,2,4096]{2,1,0:T(2,128)(2,1)S(1)}, u32[]{:S(2)}, u32[]{:S(2)}) %all-to-all-start.1) | async-done | bytes 2097184 | tf_op jit(solution)/shard_map/all_to_all | solution.py:141
  180.1 2.2 reshape.331
  182.3 2.0 fusion.72
  184.4 1.0 fusion.32
  185.4 1.7 fusion.10
  187.7 1.0 fusion.55
  188.7 367.6 %all-reduce.6 = bf16[128,4096]{1,0:T(8,128)(2,1)S(1)} all-reduce(f32[128,4096]{1,0:T(8,128)S(1)} %fusion.55), channel_id=2, replica_groups=mesh['oct'=2,'sub'=64] {'sub'}, use_global_device_ids=true, to_apply=%region_5.7.clone | all-reduce | flops 524288 | bytes 3145728
  556.3 2.0 stack.4
  558.3 5.5 all-to-all-start.2
  563.9 4.4 multiply_bitcast_fusion
  568.3 8.2 reshape.334
  577.1 0.9 all-to-all-done.2
  578.0 1.4 reshape.346
  579.4 1.3 gather_fusion.1
  580.7 1.0 broadcast_select_fusion.1
  581.8 1.0 fusion.28
  582.9 1.7 fusion.8
  587.3 20.6 %convolution_convert_fusion = bf16[256,46080]{1,0:T(8,128)(2,1)} fusion(bf16[256,256]{1,0:T(8,128)(2,1)S(1)} %bitcast.218, bf16[256,46080]{1,0:T(8,128)(2,1)} %param.18), kind=kOutput, calls=%fused_computation.7 | convolution fusion | flops 6051594240 | bytes 47316992 | tf_op jit(solution)/shard_map/while/body/eval_jaxpr/dot_general | solution.py:101
  607.9 32.9 %reshape.337 = bf16[16,16,20,2304]{3,2,1,0:T(8,128)(2,1)} reshape(bf16[256,46080]{1,0:T(8,128)(2,1)} %convolution_convert_fusion) | data formatting | bytes 47185920 | tf_op jit(solution)/shard_map/while/body/eval_jaxpr/reshape | solution.py:106
  640.8 11.5 %convolution_bitcast_fusion = bf16[16,48,2304]{2,1,0:T(8,128)(2,1)S(1)} fusion(bf16[16,16,20,2304]{3,2,1,0:T(8,128)(2,1)} %reshape.337, bf16[20,48,16]{1,2,0:T(8,128)(2,1)} %param.17), kind=kOutput, calls=%fused_computation.11 | convolution fusion | flops 1132462080 | bytes 27162624 | tf_op jit(solution)/shard_map/while/body/eval_jaxpr/bxmr,max->bar/dot_general | solution.py:107
  652.3 5.0 reshape.338
  657.4 6.0 copy.55
  663.4 5.1 reshape.339
  668.5 8.5 gather_fusion.2
  677.0 3.5 select_convert_fusion
  680.5 5.3 scatter_custom_fusion.2
  685.8 1.5 slice.52
  687.3 3.2 reshape.341
  690.4 39.2 %all_to_all.31 = bf16[128,2,4096]{2,1,0:T(2,128)(2,1)} all-to-all(bf16[128,2,4096]{2,1,0:T(2,128)(2,1)S(1)} %reshape.341), channel_id=1, replica_groups=mesh['oct'=2,'sub'=64] {'oct','sub'}, dimensions={0} | all-to-all | bytes 4194304 | tf_op jit(solution)/shard_map/all_to_all | solution.py:141
  729.6 2.7 reshape.342
  733.6 1.0 fusion.24
  734.7 1.7 fusion.6
  737.0 2.3 fusion.54
  739.3 130.5 %all-reduce.5.cloned.1.call-done = f32[128,4096]{1,0:T(8,128)} async-done(((f32[128,4096]{1,0:T(8,128)}), f32[128,4096]{1,0:T(8,128)}) %all-reduce.5.cloned.1.call-update) | async-done | bytes 2097168
  869.8 1.5 fusion.85
  871.3 1.0 stack.5
  872.3 23.1 %all_to_all.32 = bf16[64,2,4096]{2,1,0:T(2,128)(2,1)S(1)} all-to-all(bf16[64,2,4096]{2,1,0:T(2,128)(2,1)S(1)} %stack.5), channel_id=1, replica_groups=mesh['oct'=2,'sub'=64] {'sub'}, dimensions={0} | all-to-all | bytes 2097152 | tf_op jit(solution)/shard_map/all_to_all | solution.py:164
  895.7 1.6 gather_fusion.3
  897.3 1.0 broadcast_select_fusion
  898.5 1.0 fusion.20
  899.5 1.7 fusion.4
  (141 shorter events, 14.8 us)
Async XLA Ops:
  10.2 16.5 %copy-start.32 = (s32[256,1]{0,1:T(1,128)}, s32[256,1]{0,1:T(1,128)S(1)}, u32[]{:S(2)}) copy-start(s32[256,1]{0,1:T(1,128)S(1)} %compare_select_fusion.1) | copy-start | bytes 3076
  13.1 127.2 %all-to-all-start = ((bf16[128,1,2]{2,1,0:T(2,128)(2,1)}), bf16[128,1,2]{2,1,0:T(2,128)(2,1)}, u32[]{:S(2)}, u32[]{:S(2)}) async-start(bf16[128,1,2]{2,1,0:T(2,128)(2,1)} %all_to_all.25), calls=%async_computation | async-start | bytes 131072 | tf_op jit(solution)/shard_map/all_to_all | solution.py:148
  27.4 98.4 %copy-start.21 = (pred[16,16]{1,0:T(8,128)(4,1)}, pred[16,16]{1,0:T(8,128)(4,1)S(1)}, u32[]{:S(2)}) copy-start(pred[16,16]{1,0:T(8,128)(4,1)S(1)} %and_bitcast_fusion) | copy-start | bytes 772
  29.8 2.5 copy-start.11
  29.8 3.0 copy-start.10
  29.8 3.5 copy-start.8
  32.4 2.1 copy-start.4
  34.5 21.4 %copy-start.6 = (f32[256,256,1]{1,0,2:T(8,128)}, f32[256,256,1]{1,0,2:T(8,128)S(1)}, u32[]{:S(2)}) copy-start(f32[256,256,1]{1,0,2:T(8,128)S(1)} %reshape.415) | copy-start | bytes 786436
  140.3 9.9 %copy-start.12 = (f32[2,16,16]{2,1,0:T(8,128)S(1)}, f32[2,16,16]{2,1,0:T(8,128)}, u32[]{:S(2)}) copy-start(f32[2,16,16]{2,1,0:T(8,128)} %param.19) | copy-start | bytes 6148
  140.3 39.8 %all-to-all-start.1 = ((bf16[128,2,4096]{2,1,0:T(2,128)(2,1)}), bf16[128,2,4096]{2,1,0:T(2,128)(2,1)S(1)}, u32[]{:S(2)}, u32[]{:S(2)}) async-start(bf16[128,2,4096]{2,1,0:T(2,128)(2,1)} %reshape.330), calls=%async_computation.1 | async-start | bytes 4194304 | tf_op jit(solution)/shard_map/all_to_all | solution.py:141
  154.7 10.3 %copy-start.35 = (u32[128]{0:T(128)S(1)}, u32[128]{0:T(128)}, u32[]{:S(2)}) copy-start(u32[128]{0:T(128)} %constant.167) | copy-start | bytes 1540
  154.7 11.7 %copy-start.34 = (s32[16]{0:T(128)S(1)}, s32[16]{0:T(128)}, u32[]{:S(2)}) copy-start(s32[16]{0:T(128)} %param.23) | copy-start | bytes 196
  154.7 11.7 %copy-start.33 = (s32[16]{0:T(128)S(1)}, s32[16]{0:T(128)}, u32[]{:S(2)}) copy-start(s32[16]{0:T(128)} %param.22) | copy-start | bytes 196
  165.0 19.4 %copy-start = (f32[1024,256]{1,0:T(8,128)}, f32[1024,256]{1,0:T(8,128)S(1)}, u32[]{:S(2)}) copy-start(f32[1024,256]{1,0:T(8,128)S(1)} %copy.78) | copy-start | bytes 3145732
  166.4 418.2 %copy-start.25 = (pred[16]{0:T(512)(128)(4,1)}, pred[16]{0:T(512)(128)(4,1)S(1)}, u32[]{:S(2)}) copy-start(pred[16]{0:T(512)(128)(4,1)S(1)} %fusion.84) | copy-start | bytes 52
  166.5 410.6 %copy-start.30 = (s32[16]{0:T(128)}, s32[16]{0:T(128)S(1)}, u32[]{:S(2)}) copy-start(s32[16]{0:T(128)S(1)} %get-tuple-element.37) | copy-start | bytes 196
  166.5 414.2 %copy-start.28 = (pred[16]{0:T(512)(128)(4,1)}, pred[16]{0:T(512)(128)(4,1)S(1)}, u32[]{:S(2)}) copy-start(pred[16]{0:T(512)(128)(4,1)S(1)} %get-tuple-element.36) | copy-start | bytes 52
  166.6 20.5 %copy-start.17 = (f32[16,16]{1,0:T(8,128)}, f32[16,16]{1,0:T(8,128)S(1)}, u32[]{:S(2)}) copy-start(f32[16,16]{1,0:T(8,128)S(1)} %get-tuple-element.48) | copy-start | bytes 3076
  166.6 20.5 %copy-start.19 = (f32[16,16]{1,0:T(8,128)}, f32[16,16]{1,0:T(8,128)S(1)}, u32[]{:S(2)}) copy-start(f32[16,16]{1,0:T(8,128)S(1)} %get-tuple-element.49) | copy-start | bytes 3076
  167.8 16.5 %copy-start.23 = (s32[256]{0:T(256)}, s32[256]{0:T(256)S(1)}, u32[]{:S(2)}) copy-start(s32[256]{0:T(256)S(1)} %reshape.345) | copy-start | bytes 3076
  558.3 19.7 %all-to-all-start.2 = ((bf16[64,2,4096]{2,1,0:T(2,128)(2,1)}), bf16[64,2,4096]{2,1,0:T(2,128)(2,1)}, u32[]{:S(2)}, u32[]{:S(2)}) async-start(bf16[64,2,4096]{2,1,0:T(2,128)(2,1)} %stack.4), calls=%async_computation.2 | async-start | bytes 2097152 | tf_op jit(solution)/shard_map/all_to_all | solution.py:164
  563.8 305.9 %all-reduce.5.cloned.1.call-start = ((), (), s32[]{:S(2)}) async-start(), calls=%async_computation.5 | async-start | bytes 4194304
  576.9 4.9 copy-start.2
  577.0 7.6 copy-start.13
  577.1 7.6 copy-start.15
  577.1 3.6 copy-start.27
  582.9 2.5 copy-start.5
  584.6 1.7 copy-start.9
  585.2 1.2 copy-start.7
  668.5 8.5 copy-start.22
  729.6 2.8 copy-start.24
  732.4 1.2 copy-start.1
  732.8 3.6 copy-start.18
  732.8 3.6 copy-start.20
  732.8 3.6 copy-start.26
  733.6 3.4 copy-start.31
  895.4 1.9 copy-start.29
  895.7 2.7 copy-start.3
  898.4 2.9 copy-start.14
  898.4 2.9 copy-start.16
Sparse Core Ops, SparseCore 0:
  739.4 130.2 all-reduce.4
